TPU v7x, 32 devices: a whole 2x2x4 slice. The times are simulated.
32 devices in a mesh: prow: 2 (over core), pcol: 16 (over z, y, x).
Axes of the slice: x: 2, y: 2, z: 4, core: 2. Of those that a mesh axis runs over, the one named last changes fastest.
Arguments:
- factor_rows: float32 [8, 256, 24, 2048], P(None, 'prow', None, 'pcol'), as said below
- sensitivity: float32 [1024, 24, 2048], P('prow', None, 'pcol'), may hold values from -6 to 6
- pivots: int32 [2048], replicated, may hold values from 0 to 2047, as said below
Outputs:
- adjoint: float32 [1024, 8, 256], P(None, None, 'prow')
- updated: float32 [1024, 24, 2048], P('prow', None, 'pcol')
Inputs may be any that keep to these rules, and one draw needn't show every extreme that they name: pivots is a permutation of the first 2048 columns. `factor_rows`: in M, the entries left of each block row's diagonal block are zero and each diagonal block is lower triangular.
All inputs are finite; a program needn't handle non-finite values.
Results may differ from a plain program's by a relative error of at most 0.0001.
Values sent between devices are 32-bit elements; how exact they have to be, the bound alone decides.
No kernel may reach another device: no remote copies, remote signals or barrier semaphores. Data moves between devices by JAX's collectives and lax.ppermute only.
A program may use at most 192 MiB of HBM per device.

v0:
```python
import jax
import jax.numpy as jnp
from jax import lax
from jax.sharding import PartitionSpec as P

NB = 1024


def shards(factor_rows, sensitivity, pivots):
    pcol_count = lax.axis_size("pcol")
    row_cycles = factor_rows.shape[0]
    half_cycles = row_cycles // 2
    tile_width = factor_rows.shape[1]
    col_tiles = factor_rows.shape[2]
    local_rhs = sensitivity.shape[0]
    per_block = NB // tile_width
    pcol_index = lax.axis_index("pcol")
    tile_ids = jnp.arange(col_tiles) * pcol_count + pcol_index
    stripe_cols = pcol_count * tile_width
    gathered = lax.all_gather(sensitivity[:, :1, :], "pcol", axis=2, tiled=True)
    flat_cols = gathered.reshape(local_rhs, stripe_cols)
    swapped = jnp.take(flat_cols, pivots, axis=1)
    merged = swapped.reshape(local_rhs, 1, pcol_count, tile_width)
    own_tiles = lax.dynamic_index_in_dim(merged, pcol_index, 2, keepdims=False)
    working = jnp.concatenate([own_tiles, sensitivity[:, 1:, :]], axis=1)

    def tile_range(section):
        return (
            section * per_block // pcol_count,
            ((section + 1) * per_block - 1) // pcol_count + 1,
        )

    def solve_block(working, section):
        low_tile, high_tile = tile_range(section)
        chosen = tile_ids[low_tile:high_tile]
        inside = ((chosen >= section * per_block) & (chosen < (section + 1) * per_block)).astype(
            jnp.float32
        )
        masked = working[:, low_tile:high_tile, :] * inside[None, :, None]
        all_rhs = lax.all_gather(masked, "prow", axis=0, tiled=True)
        inverse_tiles = factor_rows[
            section * half_cycles : (section + 1) * half_cycles, :, low_tile:high_tile, :
        ]
        partial_sum = jnp.einsum(
            "hbu,atbu->hat",
            all_rhs,
            inverse_tiles,
            precision=lax.Precision.HIGHEST,
            preferred_element_type=jnp.float32,
        )
        partial_sum = partial_sum.reshape(all_rhs.shape[0], half_cycles * tile_width)
        return lax.psum(partial_sum, "pcol")

    solved_first = solve_block(working, 0)
    low_tile, high_tile = tile_range(1)
    next_tiles = high_tile - low_tile
    first_rows = factor_rows[:half_cycles, :, low_tile:high_tile, :].reshape(
        half_cycles * tile_width, next_tiles * tile_width
    )
    picked = solved_first
    early = lax.psum_scatter(
        jnp.dot(
            picked, first_rows, precision=lax.Precision.HIGHEST, preferred_element_type=jnp.float32
        ),
        "prow",
        scatter_dimension=0,
        tiled=True,
    ).reshape(local_rhs, next_tiles, tile_width)
    chosen = tile_ids[low_tile:high_tile]
    inside = ((chosen >= per_block) & (chosen < 2 * per_block)).astype(jnp.float32)
    working = working.at[:, low_tile:high_tile, :].add(-early * inside[None, :, None])
    solved_second = solve_block(working, 1)
    both_solved = jnp.concatenate([solved_first, solved_second], axis=1)
    all_rows = factor_rows.reshape(row_cycles * tile_width, col_tiles * tile_width)
    picked = both_solved
    change = lax.psum_scatter(
        jnp.dot(
            picked, all_rows, precision=lax.Precision.HIGHEST, preferred_element_type=jnp.float32
        ),
        "prow",
        scatter_dimension=0,
        tiled=True,
    ).reshape(local_rhs, col_tiles, tile_width)
    keep_cols = (tile_ids >= 2 * per_block).astype(jnp.float32)
    working = working - change * keep_cols[None, :, None]
    adjoint = jnp.concatenate([solved_first, solved_second], axis=1).reshape(
        solved_first.shape[0], row_cycles, tile_width
    )
    return (adjoint, working)


def solution(mesh):
    return jax.shard_map(
        shards,
        mesh=mesh,
        in_specs=(P(None, "prow", None, "pcol"), P("prow", None, "pcol"), P()),
        out_specs=(P(None, None, "prow"), P("prow", None, "pcol")),
        check_vma=False,
    )
```

profile of v0, /device:TPU:0, one launch (start us, length us, event | category | flops | bytes accessed | tf_op | source)
XLA Modules:
  0.0 478.7 jit_solution(9994754397476234976)
XLA Ops:
  7.2 1.7 slice.41
  8.9 0.8 copy.11
  9.8 0.0 all-reduce.3.cloned.1.call-start
  9.9 0.7 and_bitcast_fusion
  10.7 0.7 fusion.4
  11.4 2.5 fusion.5
  13.9 76.2 %all-gather.3.cloned.1.call-done = f32[512,1,2048]{0,2,1:T(8,128)} async-done(((f32[512,1,128]{0,2,1:T(8,128)}), f32[512,1,2048]{0,2,1:T(8,128)}) %all-gather.3.cloned.1.call-update) | async-done | bytes 4194320 | tf_op jit(solution)/shard_map/all_gather | solution.py:20
  90.2 11.7 %gather_fusion = f32[2048,512]{1,0:T(8,128)} fusion(f32[512,2048]{0,1:T(8,128)} %bitcast.40, s32[2048]{0:T(1024)S(1)} %fusion.4), kind=kCustom, calls=%fused_computation | custom fusion | bytes 8396800 | tf_op jit(solution)/shard_map/jit(_take)/gather | solution.py:22
  101.8 1.0 constant_dynamic-slice_fusion.1
  102.8 0.1 copy.12
  103.0 2.2 all_gather.10
  105.2 3.1 fusion.6
  108.3 0.0 reduce-scatter.3.cloned.1.call-start
  108.4 124.7 %all-reduce.3.cloned.1.call-done = f32[1024,512]{1,0:T(8,128)} async-done(((f32[1024,512]{1,0:T(8,128)}), f32[1024,512]{1,0:T(8,128)}) %all-reduce.3.cloned.1.call-update) | async-done | bytes 2097168 | tf_op jit(solution)/shard_map/psum | solution.py:52
  233.0 4.2 fusion.7
  237.2 0.0 all-reduce.5.cloned.1.call-start
  237.4 7.3 %reduce-scatter.3.cloned.1.call-done = f32[512,128]{1,0:T(8,128)} async-done(((f32[1024,128]{1,0:T(8,128)}), f32[512,128]{1,0:T(8,128)}) %reduce-scatter.3.cloned.1.call-update) | async-done | bytes 262160 | tf_op jit(solution)/shard_map/reduce_scatter | solution.py:61
  244.7 1.0 broadcast_multiply_fusion
  245.7 2.2 all-gather
  247.9 3.1 fusion.8
  251.0 0.2 reduce-scatter.5.cloned.1.call-start
  251.2 1.6 constant_dynamic-update-slice_fusion.1
  252.8 125.4 %all-reduce.5.cloned.1.call-done = f32[1024,512]{1,0:T(8,128)} async-done(((f32[1024,512]{1,0:T(8,128)}), f32[1024,512]{1,0:T(8,128)}) %all-reduce.5.cloned.1.call-update) | async-done | bytes 2097168 | tf_op jit(solution)/shard_map/psum | solution.py:52
  378.3 3.2 constant_dynamic-update-slice_fusion
  381.4 60.8 %fusion = f32[1024,3072]{1,0:T(8,128)} fusion(f32[1024,1024]{1,0:T(8,128)} %constant_dynamic-update-slice_fusion, f32[128,8,24,128]{3,2,1,0:T(8,128)} %bitcast.55), kind=kOutput, calls=%fused_computation.1 | convolution fusion | flops 38654705664 | bytes 29360128 | tf_op jit(solution)/shard_map/dot_general | solution.py:77
  442.2 3.4 slice.45
  445.6 4.0 pad_maximum_fusion
  449.6 8.2 %scatter-add.4 = f32[512,24,128]{2,1,0:T(8,128)} dynamic-update-slice(f32[512,24,128]{2,1,0:T(8,128)} %pad_maximum_fusion, f32[512,1,128]{2,1,0:T(1,128)S(1)} %bitcast.52, s32[]{:T(128)} %constant.48.clone.1, s32[]{:T(128)} %constant.48.clone.1, s32[]{:T(128)} %constant.48.clone.1) | dynamic-update-slice | bytes 524292 | tf_op jit(solution)/shard_map/scatter-add | solution.py:71
  457.8 6.1 %copy.13 = f32[128,8,8,128]{3,2,1,0:T(8,128)} copy(f32[128,8,8,128]{3,1,2,0:T(8,128)} %bitcast.43) | data formatting | bytes 8388608
  464.0 4.3 copy.15
  468.3 0.3 slice-done.1
  468.6 3.6 fusion.3
  (18 shorter events, 0.2 us)
Async XLA Ops:
  7.2 83.0 %all-gather.3.cloned.1.call-start = ((), (), s32[]{:S(2)}) async-start(), calls=%async_computation.2 | async-start | bytes 4456448 | tf_op jit(solution)/shard_map/all_gather | solution.py:20
  9.8 223.2 %all-reduce.3.cloned.1.call-start = ((), (), s32[]{:S(2)}) async-start(), calls=%async_computation.3 | async-start | bytes 4194304 | tf_op jit(solution)/shard_map/psum | solution.py:52
  108.3 136.4 %reduce-scatter.3.cloned.1.call-start = ((), (), s32[]{:S(2)}) async-start(), calls=%async_computation.4 | async-start | bytes 786432 | tf_op jit(solution)/shard_map/reduce_scatter | solution.py:61
  237.2 14.0 %copy-start = (f32[1024,512]{1,0:T(8,128)S(1)}, f32[1024,512]{1,0:T(8,128)}, u32[]{:S(2)}) copy-start(f32[1024,512]{1,0:T(8,128)} %all-reduce.3.cloned.1.call-done) | copy-start | bytes 6291460
  237.2 141.0 %all-reduce.5.cloned.1.call-start = ((), (), s32[]{:S(2)}) async-start(), calls=%async_computation.5 | async-start | bytes 4194304 | tf_op jit(solution)/shard_map/psum | solution.py:52
  251.0 213.0 %reduce-scatter.5.cloned.1.call-start = ((), (), s32[]{:S(2)}) async-start(), calls=%async_computation.6 | async-start | bytes 18874368 | tf_op jit(solution)/shard_map/reduce_scatter | solution.py:76
  464.0 4.4 slice-start
  464.0 4.7 slice-start.1
Sparse Core Ops, SparseCore 0:
  11.3 78.7 all-gather.2
  108.4 124.5 all-reduce.2
  237.4 7.2 reduce-scatter.2
  251.1 127.1 all-reduce.4
  442.4 20.8 reduce-scatter.4
where the time goes:
time: 479 us
  waiting for transfers between devices  334 us (70%)
  matrix products  71.2 us (15%)
  local copies, waits for them, and re-layouts  45.1 us (9%)
  between operations  14 us (3%)
  other arithmetic  9.97 us (2%)
    psum x2, waiting for transfers between devices, solve_block(): return lax.psum(partial_sum, 'pcol')  250 us
    all_gather x1, waiting for transfers between devices, shards(): gathered = lax.all_gather(sensitivity[:, :1, :], 'pcol', axis=2, tiled=True)  76.2 us
    dot_general x1, matrix products, shards(): jnp.dot(picked, all_rows, precision=lax.Precision.HIGHEST, preferred_elem...  60.8 us
    unnamed x11, local copies, waits for them, and re-layouts  13.4 us
    gather x1, local copies, waits for them, and re-layouts, shards(): swapped = jnp.take(flat_cols, pivots, axis=1)  11.7 us
  transfers between devices with their start and end apart: 5, of which 4 were waited for; matrix products, arithmetic and copies ran while one was open for 6% of the time, Pallas kernels for 0%

commit v1 on v0

--- a/solution.py
+++ b/solution.py
@@ -17,7 +17,22 @@
     pcol_index = lax.axis_index("pcol")
     tile_ids = jnp.arange(col_tiles) * pcol_count + pcol_index
     stripe_cols = pcol_count * tile_width
-    gathered = lax.all_gather(sensitivity[:, :1, :], "pcol", axis=2, tiled=True)
+    x = sensitivity[:, :1, :]
+    ways, here, step = (lax.axis_size("pcol"), lax.axis_index("pcol"), x.shape[2])
+    shape = [n * ways if d == 2 else n for d, n in enumerate(x.shape)]
+    full = lax.dynamic_update_slice_in_dim(jnp.zeros(shape, x.dtype), x, here * step, axis=2)
+    going_up = going_down = x
+    for far in range(1, ways // 2 + 1):
+        going_up = lax.ppermute(going_up, "pcol", [(d, (d + 1) % ways) for d in range(ways)])
+        full = lax.dynamic_update_slice_in_dim(full, going_up, (here - far) % ways * step, axis=2)
+        if 2 * far < ways:
+            going_down = lax.ppermute(
+                going_down, "pcol", [(d, (d - 1) % ways) for d in range(ways)]
+            )
+            full = lax.dynamic_update_slice_in_dim(
+                full, going_down, (here + far) % ways * step, axis=2
+            )
+    gathered = full
     flat_cols = gathered.reshape(local_rhs, stripe_cols)
     swapped = jnp.take(flat_cols, pivots, axis=1)
     merged = swapped.reshape(local_rhs, 1, pcol_count, tile_width)

time: 479 us -> 506 us (1.056)
  starting transfers between devices: 0.39 us -> 48.9 us
  waiting for transfers between devices: 334 us -> 298 us
  local copies, waits for them, and re-layouts: 45.1 us -> 58.4 us
    all_gather x1 -> x0, waiting for transfers between devices: 76.2 us -> none  [shards(): gathered = lax.all_gather(sensitivity[:, :1, :], 'pcol', axis=2, tiled=True)]
    ppermute x0 -> x15, starting transfers between devices: none -> 48.6 us  [the longest x7 35.8 us: shards(): lax.ppermute(going_down, 'pcol', [(d, (d - 1) % ways) for d in range(ways)])]
    ppermute x0 -> x15, waiting for transfers between devices: none -> 42.9 us  [the longest x8 42.9 us: shards(): lax.ppermute(going_up, 'pcol', [(d, (d + 1) % ways) for d in range(ways)])]
    dynamic_update_slice x0 -> x16, local copies, waits for them, and re-layouts: none -> 11.5 us  [the longest x8 5.75 us: shards(): lax.dynamic_update_slice_in_dim(full, going_up, (here - far) % ways * ste...]
  transfers between devices with their start and end apart: 5 -> 19, of which waited for: 4 -> 11; matrix products, arithmetic and copies ran while one was open for 6% -> 8% of each run, Pallas kernels for 0% -> 0%
where the time goes in v1:
time: 506 us; the launch traced here: 505 us
  waiting for transfers between devices  298 us (59%)
  matrix products  71.2 us (14%)
  local copies, waits for them, and re-layouts  58.4 us (12%)
  starting transfers between devices  48.9 us (10%)
  between operations  14.3 us (3%)
  other arithmetic  9.97 us (2%)
    psum x2, waiting for transfers between devices, solve_block(): return lax.psum(partial_sum, 'pcol')  247 us
    dot_general x1, matrix products, shards(): jnp.dot(picked, all_rows, precision=lax.Precision.HIGHEST, preferred_elem...  60.8 us
    ppermute x8, waiting for transfers between devices, shards(): lax.ppermute(going_up, 'pcol', [(d, (d + 1) % ways) for d in range(ways)])  42.9 us
    ppermute x7, starting transfers between devices, shards(): lax.ppermute(going_down, 'pcol', [(d, (d - 1) % ways) for d in range(ways)])  35.8 us
    ppermute x8, starting transfers between devices, shards(): lax.ppermute(going_up, 'pcol', [(d, (d + 1) % ways) for d in range(ways)])  12.8 us
    unnamed x11, local copies, waits for them, and re-layouts  12.6 us
    gather x1, local copies, waits for them, and re-layouts, shards(): swapped = jnp.take(flat_cols, pivots, axis=1)  11.7 us
  transfers between devices with their start and end apart: 19, of which 11 were waited for; matrix products, arithmetic and copies ran while one was open for 8% of the time, Pallas kernels for 0%

profile of v1, /device:TPU:0, one launch (start us, length us, event | category | flops | bytes accessed | tf_op | source)
XLA Modules:
  0.0 504.9 jit_solution(3268297694399719007)
XLA Ops:
  9.1 7.0 %collective-permute-start.1 = (f32[512,1,128]{0,2,1:T(8,128)S(1)}, f32[512,1,128]{0,2,1:T(8,128)S(1)}, u32[]{:S(2)}, u32[]{:S(2)}) collective-permute-start(f32[512,1,128]{0,2,1:T(8,128)S(1)} %copy.11), channel_id=1, source_target_pairs={{0,15},{1,0},{2,1},{3,2},{4,3},{5,4},{6,5},{7,6},{8,7},{9,8},{10,9... | collective-permute-start | bytes 786440 | tf_op jit(solution)/shard_map/ppermute | solution.py:29
  17.5 2.5 fusion.5
  20.4 2.5 reshape.184
  23.7 5.6 %collective-permute-start.3 = (f32[512,1,128]{0,2,1:T(8,128)S(1)}, f32[512,1,128]{0,2,1:T(8,128)S(1)}, u32[]{:S(2)}, u32[]{:S(2)}) collective-permute-start(f32[512,1,128]{0,2,1:T(8,128)S(1)} %collective-permute-done.1), channel_id=1, source_target_pairs={{0,15},{1,0},{2,1},{3,2},{4,3},{5,4},{6,5},{7,6},{8,7},{9,8},{10,9... | collective-permute-start | bytes 786440 | tf_op jit(solution)/shard_map/ppermute | solution.py:29
  34.6 5.9 %collective-permute-start.5 = (f32[512,1,128]{0,2,1:T(8,128)S(1)}, f32[512,1,128]{0,2,1:T(8,128)S(1)}, u32[]{:S(2)}, u32[]{:S(2)}) collective-permute-start(f32[512,1,128]{0,2,1:T(8,128)S(1)} %collective-permute-done.3), channel_id=1, source_target_pairs={{0,15},{1,0},{2,1},{3,2},{4,3},{5,4},{6,5},{7,6},{8,7},{9,8},{10,9... | collective-permute-start | bytes 786440 | tf_op jit(solution)/shard_map/ppermute | solution.py:29
  40.6 4.0 collective-permute-done.2
  44.6 2.5 collective-permute-start.4
  48.5 4.9 collective-permute-start.7
  53.4 4.2 collective-permute-done.4
  61.5 4.7 collective-permute-start.9
  66.2 4.4 collective-permute-done.6
  74.5 4.5 collective-permute-start.11
  79.0 6.4 %collective-permute-done.8 = f32[512,1,128]{0,2,1:T(8,128)S(1)} collective-permute-done((f32[512,1,128]{0,2,1:T(8,128)S(1)}, f32[512,1,128]{0,2,1:T(8,128)S(1)}, u32[]{:S(2)}, u32[]{:S(2)}) %collective-permute-start.8) | collective-permute-done | bytes 262176 | tf_op jit(solution)/shard_map/ppermute | solution.py:26
  89.4 3.1 collective-permute-start.13
  92.5 4.8 collective-permute-done.10
  99.2 9.1 %collective-permute-done.12 = f32[512,1,128]{0,2,1:T(8,128)S(1)} collective-permute-done((f32[512,1,128]{0,2,1:T(8,128)S(1)}, f32[512,1,128]{0,2,1:T(8,128)S(1)}, u32[]{:S(2)}, u32[]{:S(2)}) %collective-permute-start.12) | collective-permute-done | bytes 262176 | tf_op jit(solution)/shard_map/ppermute | solution.py:26
  109.7 8.6 %collective-permute-done.14 = f32[512,1,128]{0,2,1:T(8,128)S(1)} collective-permute-done((f32[512,1,128]{0,2,1:T(8,128)S(1)}, f32[512,1,128]{0,2,1:T(8,128)S(1)}, u32[]{:S(2)}, u32[]{:S(2)}) %collective-permute-start.14) | collective-permute-done | bytes 262176 | tf_op jit(solution)/shard_map/ppermute | solution.py:26
  119.0 11.7 %gather_fusion = f32[2048,512]{1,0:T(8,128)} fusion(f32[512,2048]{0,1:T(8,128)} %bitcast_dynamic-update-slice_fusion, s32[2048]{0:T(1024)S(1)} %fusion.4), kind=kCustom, calls=%fused_computation | custom fusion | bytes 8396800 | tf_op jit(solution)/shard_map/jit(_take)/gather | solution.py:37
  134.0 3.1 fusion.6
  137.2 122.0 %all-reduce.3.cloned.1.call-done = f32[1024,512]{1,0:T(8,128)} async-done(((f32[1024,512]{1,0:T(8,128)}), f32[1024,512]{1,0:T(8,128)}) %all-reduce.3.cloned.1.call-update) | async-done | bytes 2097168 | tf_op jit(solution)/shard_map/psum | solution.py:67
  259.2 4.2 fusion.7
  263.5 7.3 %reduce-scatter.3.cloned.1.call-done = f32[512,128]{1,0:T(8,128)} async-done(((f32[1024,128]{1,0:T(8,128)}), f32[512,128]{1,0:T(8,128)}) %reduce-scatter.3.cloned.1.call-update) | async-done | bytes 262160 | tf_op jit(solution)/shard_map/reduce_scatter | solution.py:76
  274.0 3.1 fusion.8
  279.0 125.5 %all-reduce.5.cloned.1.call-done = f32[1024,512]{1,0:T(8,128)} async-done(((f32[1024,512]{1,0:T(8,128)}), f32[1024,512]{1,0:T(8,128)}) %all-reduce.5.cloned.1.call-update) | async-done | bytes 2097168 | tf_op jit(solution)/shard_map/psum | solution.py:67
  404.5 3.2 constant_dynamic-update-slice_fusion
  407.6 60.8 %fusion = f32[1024,3072]{1,0:T(8,128)} fusion(f32[1024,1024]{1,0:T(8,128)} %constant_dynamic-update-slice_fusion, f32[128,8,24,128]{3,2,1,0:T(8,128)} %bitcast.85), kind=kOutput, calls=%fused_computation.1 | convolution fusion | flops 38654705664 | bytes 29360128 | tf_op jit(solution)/shard_map/dot_general | solution.py:92
  468.4 3.4 slice.45
  471.8 4.0 pad_maximum_fusion
  475.8 8.2 %scatter-add.4 = f32[512,24,128]{2,1,0:T(8,128)} dynamic-update-slice(f32[512,24,128]{2,1,0:T(8,128)} %pad_maximum_fusion, f32[512,1,128]{2,1,0:T(1,128)S(1)} %bitcast.82, s32[]{:T(128)} %constant.150.clone.1, s32[]{:T(128)} %constant.150.clone.1, s32[]{:T(128)} %constant.150.clone.1) | dynamic-update-slice | bytes 524292 | tf_op jit(solution)/shard_map/scatter-add | solution.py:86
  484.0 6.1 %copy.13 = f32[128,8,8,128]{3,2,1,0:T(8,128)} copy(f32[128,8,8,128]{3,1,2,0:T(8,128)} %bitcast.73) | data formatting | bytes 8388608
  490.2 4.3 copy.15
  494.8 3.6 fusion.3
  (62 shorter events, 35.4 us)
Async XLA Ops:
  7.2 252.0 %all-reduce.3.cloned.1.call-start = ((), (), s32[]{:S(2)}) async-start(), calls=%async_computation.2 | async-start | bytes 4194304 | tf_op jit(solution)/shard_map/psum | solution.py:67
  9.1 14.6 %collective-permute-start.1 = (f32[512,1,128]{0,2,1:T(8,128)S(1)}, f32[512,1,128]{0,2,1:T(8,128)S(1)}, u32[]{:S(2)}, u32[]{:S(2)}) collective-permute-start(f32[512,1,128]{0,2,1:T(8,128)S(1)} %copy.11), channel_id=1, source_target_pairs={{0,15},{1,0},{2,1},{3,2},{4,3},{5,4},{6,5},{7,6},{8,7},{9,8},{10,9... | collective-permute-start | bytes 786440 | tf_op jit(solution)/shard_map/ppermute | solution.py:29
  16.1 14.7 %collective-permute-start = (f32[512,1,128]{0,2,1:T(8,128)S(1)}, f32[512,1,128]{0,2,1:T(8,128)S(1)}, u32[]{:S(2)}, u32[]{:S(2)}) collective-permute-start(f32[512,1,128]{0,2,1:T(8,128)S(1)} %copy.11), channel_id=1, source_target_pairs={{0,1},{1,2},{2,3},{3,4},{4,5},{5,6},{6,7},{7,8},{8,9},{9,10},{10,1... | collective-permute-start | bytes 786440 | tf_op jit(solution)/shard_map/ppermute | solution.py:26
  23.7 11.0 %collective-permute-start.3 = (f32[512,1,128]{0,2,1:T(8,128)S(1)}, f32[512,1,128]{0,2,1:T(8,128)S(1)}, u32[]{:S(2)}, u32[]{:S(2)}) collective-permute-start(f32[512,1,128]{0,2,1:T(8,128)S(1)} %collective-permute-done.1), channel_id=1, source_target_pairs={{0,15},{1,0},{2,1},{3,2},{4,3},{5,4},{6,5},{7,6},{8,7},{9,8},{10,9... | collective-permute-start | bytes 786440 | tf_op jit(solution)/shard_map/ppermute | solution.py:29
  30.8 13.8 %collective-permute-start.2 = (f32[512,1,128]{0,2,1:T(8,128)S(1)}, f32[512,1,128]{0,2,1:T(8,128)S(1)}, u32[]{:S(2)}, u32[]{:S(2)}) collective-permute-start(f32[512,1,128]{0,2,1:T(8,128)S(1)} %collective-permute-done), channel_id=1, source_target_pairs={{0,1},{1,2},{2,3},{3,4},{4,5},{5,6},{6,7},{7,8},{8,9},{9,10},{10,1... | collective-permute-start | bytes 786440 | tf_op jit(solution)/shard_map/ppermute | solution.py:26
  34.6 13.8 %collective-permute-start.5 = (f32[512,1,128]{0,2,1:T(8,128)S(1)}, f32[512,1,128]{0,2,1:T(8,128)S(1)}, u32[]{:S(2)}, u32[]{:S(2)}) collective-permute-start(f32[512,1,128]{0,2,1:T(8,128)S(1)} %collective-permute-done.3), channel_id=1, source_target_pairs={{0,15},{1,0},{2,1},{3,2},{4,3},{5,4},{6,5},{7,6},{8,7},{9,8},{10,9... | collective-permute-start | bytes 786440 | tf_op jit(solution)/shard_map/ppermute | solution.py:29
  44.6 13.0 %collective-permute-start.4 = (f32[512,1,128]{0,2,1:T(8,128)S(1)}, f32[512,1,128]{0,2,1:T(8,128)S(1)}, u32[]{:S(2)}, u32[]{:S(2)}) collective-permute-start(f32[512,1,128]{0,2,1:T(8,128)S(1)} %collective-permute-done.2), channel_id=1, source_target_pairs={{0,1},{1,2},{2,3},{3,4},{4,5},{5,6},{6,7},{7,8},{8,9},{9,10},{10,1... | collective-permute-start | bytes 786440 | tf_op jit(solution)/shard_map/ppermute | solution.py:26
  48.5 13.0 %collective-permute-start.7 = (f32[512,1,128]{0,2,1:T(8,128)S(1)}, f32[512,1,128]{0,2,1:T(8,128)S(1)}, u32[]{:S(2)}, u32[]{:S(2)}) collective-permute-start(f32[512,1,128]{0,2,1:T(8,128)S(1)} %collective-permute-done.5), channel_id=1, source_target_pairs={{0,15},{1,0},{2,1},{3,2},{4,3},{5,4},{6,5},{7,6},{8,7},{9,8},{10,9... | collective-permute-start | bytes 786440 | tf_op jit(solution)/shard_map/ppermute | solution.py:29
  57.5 13.0 %collective-permute-start.6 = (f32[512,1,128]{0,2,1:T(8,128)S(1)}, f32[512,1,128]{0,2,1:T(8,128)S(1)}, u32[]{:S(2)}, u32[]{:S(2)}) collective-permute-start(f32[512,1,128]{0,2,1:T(8,128)S(1)} %collective-permute-done.4), channel_id=1, source_target_pairs={{0,1},{1,2},{2,3},{3,4},{4,5},{5,6},{6,7},{7,8},{8,9},{9,10},{10,1... | collective-permute-start | bytes 786440 | tf_op jit(solution)/shard_map/ppermute | solution.py:26
  61.5 13.0 %collective-permute-start.9 = (f32[512,1,128]{0,2,1:T(8,128)S(1)}, f32[512,1,128]{0,2,1:T(8,128)S(1)}, u32[]{:S(2)}, u32[]{:S(2)}) collective-permute-start(f32[512,1,128]{0,2,1:T(8,128)S(1)} %collective-permute-done.7), channel_id=1, source_target_pairs={{0,15},{1,0},{2,1},{3,2},{4,3},{5,4},{6,5},{7,6},{8,7},{9,8},{10,9... | collective-permute-start | bytes 786440 | tf_op jit(solution)/shard_map/ppermute | solution.py:29
  70.6 14.9 %collective-permute-start.8 = (f32[512,1,128]{0,2,1:T(8,128)S(1)}, f32[512,1,128]{0,2,1:T(8,128)S(1)}, u32[]{:S(2)}, u32[]{:S(2)}) collective-permute-start(f32[512,1,128]{0,2,1:T(8,128)S(1)} %collective-permute-done.6), channel_id=1, source_target_pairs={{0,1},{1,2},{2,3},{3,4},{4,5},{5,6},{6,7},{7,8},{8,9},{9,10},{10,1... | collective-permute-start | bytes 786440 | tf_op jit(solution)/shard_map/ppermute | solution.py:26
  74.5 14.9 %collective-permute-start.11 = (f32[512,1,128]{0,2,1:T(8,128)S(1)}, f32[512,1,128]{0,2,1:T(8,128)S(1)}, u32[]{:S(2)}, u32[]{:S(2)}) collective-permute-start(f32[512,1,128]{0,2,1:T(8,128)S(1)} %collective-permute-done.9), channel_id=1, source_target_pairs={{0,15},{1,0},{2,1},{3,2},{4,3},{5,4},{6,5},{7,6},{8,7},{9,8},{10,9... | collective-permute-start | bytes 786440 | tf_op jit(solution)/shard_map/ppermute | solution.py:29
  85.4 11.9 %collective-permute-start.10 = (f32[512,1,128]{0,2,1:T(8,128)S(1)}, f32[512,1,128]{0,2,1:T(8,128)S(1)}, u32[]{:S(2)}, u32[]{:S(2)}) collective-permute-start(f32[512,1,128]{0,2,1:T(8,128)S(1)} %collective-permute-done.8), channel_id=1, source_target_pairs={{0,1},{1,2},{2,3},{3,4},{4,5},{5,6},{6,7},{7,8},{8,9},{9,10},{10,1... | collective-permute-start | bytes 786440 | tf_op jit(solution)/shard_map/ppermute | solution.py:26
  89.4 19.6 %collective-permute-start.13 = (f32[512,1,128]{0,2,1:T(8,128)S(1)}, f32[512,1,128]{0,2,1:T(8,128)S(1)}, u32[]{:S(2)}, u32[]{:S(2)}) collective-permute-start(f32[512,1,128]{0,2,1:T(8,128)S(1)} %collective-permute-done.11), channel_id=1, source_target_pairs={{0,15},{1,0},{2,1},{3,2},{4,3},{5,4},{6,5},{7,6},{8,7},{9,8},{10,9... | collective-permute-start | bytes 786440 | tf_op jit(solution)/shard_map/ppermute | solution.py:29
  97.3 10.9 %collective-permute-start.12 = (f32[512,1,128]{0,2,1:T(8,128)S(1)}, f32[512,1,128]{0,2,1:T(8,128)S(1)}, u32[]{:S(2)}, u32[]{:S(2)}) collective-permute-start(f32[512,1,128]{0,2,1:T(8,128)S(1)} %collective-permute-done.10), channel_id=1, source_target_pairs={{0,1},{1,2},{2,3},{3,4},{4,5},{5,6},{6,7},{7,8},{8,9},{9,10},{10,1... | collective-permute-start | bytes 786440 | tf_op jit(solution)/shard_map/ppermute | solution.py:26
  108.3 10.0 %collective-permute-start.14 = (f32[512,1,128]{0,2,1:T(8,128)S(1)}, f32[512,1,128]{0,2,1:T(8,128)S(1)}, u32[]{:S(2)}, u32[]{:S(2)}) collective-permute-start(f32[512,1,128]{0,2,1:T(8,128)S(1)} %collective-permute-done.12), channel_id=1, source_target_pairs={{0,1},{1,2},{2,3},{3,4},{4,5},{5,6},{6,7},{7,8},{8,9},{9,10},{10,1... | collective-permute-start | bytes 786440 | tf_op jit(solution)/shard_map/ppermute | solution.py:26
  137.2 133.7 %reduce-scatter.3.cloned.1.call-start = ((), (), s32[]{:S(2)}) async-start(), calls=%async_computation.3 | async-start | bytes 786432 | tf_op jit(solution)/shard_map/reduce_scatter | solution.py:76
  263.4 14.0 %copy-start = (f32[1024,512]{1,0:T(8,128)S(1)}, f32[1024,512]{1,0:T(8,128)}, u32[]{:S(2)}) copy-start(f32[1024,512]{1,0:T(8,128)} %all-reduce.3.cloned.1.call-done) | copy-start | bytes 6291460
  263.4 141.1 %all-reduce.5.cloned.1.call-start = ((), (), s32[]{:S(2)}) async-start(), calls=%async_computation.4 | async-start | bytes 4194304 | tf_op jit(solution)/shard_map/psum | solution.py:67
  277.2 213.0 %reduce-scatter.5.cloned.1.call-start = ((), (), s32[]{:S(2)}) async-start(), calls=%async_computation.5 | async-start | bytes 18874368 | tf_op jit(solution)/shard_map/reduce_scatter | solution.py:91
  490.2 4.4 slice-start
  490.2 4.7 slice-start.1
Sparse Core Ops, SparseCore 0:
  137.3 121.8 all-reduce.2
  263.5 7.2 reduce-scatter.2
  277.3 127.1 all-reduce.4
  468.6 20.8 reduce-scatter.4
